TPU v7x, 128 devices: a whole 4x4x4 slice. The times are simulated.
128 devices in a mesh: img: 2 (over core), band: 64 (over z, y, x).
Axes of the slice: x: 4, y: 4, z: 4, core: 2. Of those that a mesh axis runs over, the one named last changes fastest.
Arguments:
- latent: bfloat16 [8, 256, 32, 1280], P('img', 'band'), parts along dimension 0, may hold values from -80 to 80
- stale_act: bfloat16 [8, 256, 32, 1280], P('img', 'band'), parts along dimension 0, may hold values from -4 to 4
- stale_kv: bfloat16 [2, 8, 256, 32, 640], P(None, 'img', 'band'), parts along dimension 1, may hold values from -600 to 600
- timestep: int32 [8, 8], P('img'), parts along dimension 0, may hold values from 0 to 999
- norm_gain: float32 [1280], replicated, may hold values from 0.1 to 1.9
- norm_shift: float32 [1280], replicated, may hold values from -1 to 1
- conv_weight: bfloat16 [3, 3, 1280, 640], replicated, may hold values from -0.0546875 to 0.0546875
- time_weight: bfloat16 [1280, 640], replicated, may hold values from -0.15625 to 0.15625
- attn_in: bfloat16 [1280, 1920], replicated, may hold values from -0.15625 to 0.15625
- attn_out: bfloat16 [640, 1280], replicated, may hold values from -0.25 to 0.25
Outputs:
- block_out: bfloat16 [8, 256, 32, 1280], P('img', 'band'), parts along dimension 0
- fresh_kv: bfloat16 [2, 8, 256, 32, 640], P(None, 'img', 'band'), parts along dimension 1
There are 2 independent parts, one for each index of `img`. A program takes and returns all parts, laid end to end along the dimension named above; an argument that names none is the same for every part. Nothing has to cross between parts.
All inputs are finite; a program needn't handle non-finite values.
Results may differ from a plain program's by a relative error of at most 0.0055.
Values may be sent and summed in bfloat16 or wider, within the bound.
No kernel may reach another device: no remote copies, remote signals or barrier semaphores. Data moves between devices by JAX's collectives and lax.ppermute only.
A program may use at most 192 MiB of HBM per device.

v0:
```python
import math
import jax
import jax.numpy as jnp
from jax import lax
from jax.sharding import PartitionSpec as P

IMG_ROWS = 32
GROUPS = 32
HEADS = 10
TDIM = 1280


def shifted(value, axis, by):
    count = lax.axis_size(axis)
    pairs = [(i, i + by) for i in range(count) if 0 <= i + by < count]
    return lax.ppermute(value, axis, pairs)


def time_term(timestep, time_weight):
    half_dim = TDIM // 2
    frequency = jnp.exp(-math.log(10000.0) * jnp.arange(half_dim, dtype=jnp.float32) / half_dim)
    angles = timestep.astype(jnp.float32)[:, None] * frequency[None, :]
    embedding = jnp.concatenate([jnp.cos(angles), jnp.sin(angles)], axis=1)
    return jnp.dot(
        jax.nn.silu(embedding), time_weight.astype(jnp.float32), precision=lax.Precision.HIGHEST
    )


def attend_block(queries, keys, values, scale_factor):
    scores = (
        jnp.einsum("bqhd,bkhd->bhqk", queries, keys, preferred_element_type=jnp.float32)
        * scale_factor
    )
    peak = jnp.max(scores, axis=-1)
    exponent = jnp.exp(scores - peak[..., None])
    context = jnp.einsum(
        "bhqk,bkhd->bhqd", exponent.astype(jnp.bfloat16), values, preferred_element_type=jnp.float32
    )
    return (peak, jnp.sum(exponent, axis=-1), context)


def on_device(
    latent,
    stale_act,
    stale_kv,
    timestep,
    norm_gain,
    norm_shift,
    conv_weight,
    time_weight,
    attn_in,
    attn_out,
):
    images, height, columns, channels = latent.shape
    conv_width = conv_weight.shape[3]
    inner_width = attn_out.shape[0]
    head_count = HEADS
    head_size = inner_width // head_count
    per_group = channels // GROUPS
    group_size = IMG_ROWS // height
    band_count = lax.axis_size("band")
    stacked = band_count * height // IMG_ROWS
    band_index = lax.axis_index("band")
    slot = band_index % stacked
    place = band_index // stacked
    slot_mask = (jnp.arange(stacked) == slot).astype(jnp.float32)[:, None, None]
    counted = float(IMG_ROWS * columns * per_group)
    floats = latent.astype(jnp.float32)
    grouped = floats.reshape(images, height * columns, GROUPS, per_group)
    totals = lax.psum(slot_mask * jnp.sum(grouped, axis=(1, 3))[None], "band")
    center = jnp.sum(totals * slot_mask, axis=0) / counted
    deviation = grouped - center[:, None, :, None]
    spreads = lax.psum(slot_mask * jnp.sum(deviation * deviation, axis=(1, 3))[None], "band")
    spread = jnp.sum(spreads * slot_mask, axis=0) / counted
    normed = (
        (grouped - center[:, None, :, None]) / jnp.sqrt(spread + 1e-05)[:, None, :, None]
    ).reshape(latent.shape)
    activated = jax.nn.silu(normed * norm_gain + norm_shift).astype(jnp.bfloat16)
    top_rim = shifted(stale_act[:, height - 1 :], "band", stacked)
    bottom_rim = shifted(stale_act[:, :1], "band", -stacked)
    top_rim = jnp.where(place == 0, jnp.zeros_like(top_rim), top_rim)
    bottom_rim = jnp.where(place == group_size - 1, jnp.zeros_like(bottom_rim), bottom_rim)
    extended = jnp.concatenate([top_rim, activated, bottom_rim], axis=1)
    padded = jnp.pad(extended, ((0, 0), (0, 0), (1, 1), (0, 0)))
    convolved = jnp.zeros((images, height, columns, conv_width), jnp.float32)
    for row_tap in range(3):
        for col_tap in range(3):
            convolved = convolved + jnp.einsum(
                "bhwc,cd->bhwd",
                padded[:, row_tap : row_tap + height, col_tap : col_tap + columns],
                conv_weight[row_tap, col_tap],
                preferred_element_type=jnp.float32,
            )
    own_steps = lax.dynamic_index_in_dim(timestep, slot, 1, keepdims=False)
    time_bias = time_term(own_steps, time_weight)
    window = (floats[..., :conv_width] + convolved + time_bias[:, None, None, :]).astype(
        jnp.bfloat16
    )
    hidden = jnp.concatenate([window, latent[..., conv_width:]], axis=-1)
    widened = hidden.astype(jnp.float32)
    token_mean = jnp.mean(widened, axis=-1, keepdims=True)
    token_var = jnp.mean((widened - token_mean) ** 2, axis=-1, keepdims=True)
    normalized = ((widened - token_mean) / jnp.sqrt(token_var + 1e-05)).astype(jnp.bfloat16)
    projected = jnp.dot(
        normalized.reshape(-1, channels), attn_in, preferred_element_type=jnp.float32
    )
    projected = projected.astype(jnp.bfloat16).reshape(images, height, columns, 3 * inner_width)
    fresh_kv = jnp.stack(
        [projected[..., inner_width : 2 * inner_width], projected[..., 2 * inner_width :]]
    )
    tokens_dev = height * columns
    query_heads = projected[..., :inner_width].reshape(images, tokens_dev, head_count, head_size)
    fresh_keys = fresh_kv[0].reshape(images, tokens_dev, head_count, head_size)
    fresh_values = fresh_kv[1].reshape(images, tokens_dev, head_count, head_size)
    scale_factor = head_size ** (-0.5)
    start_carry = attend_block(query_heads, fresh_keys, fresh_values, scale_factor)

    def absorb(carry, piece):
        running_max, running_sum, context = carry
        piece_rows = piece.shape[2]
        piece_keys = piece[0].reshape(images, piece_rows * columns, head_count, head_size)
        piece_values = piece[1].reshape(images, piece_rows * columns, head_count, head_size)
        peak, total, partial_ctx = attend_block(query_heads, piece_keys, piece_values, scale_factor)
        new_max = jnp.maximum(running_max, peak)
        old_factor = jnp.exp(running_max - new_max)
        new_factor = jnp.exp(peak - new_max)
        return (
            new_max,
            running_sum * old_factor + total * new_factor,
            context * old_factor[..., None] + partial_ctx * new_factor[..., None],
        )

    def chain_step(step, state):
        upward, downward, carry = state
        upward = shifted(upward, "band", stacked)
        downward = shifted(downward, "band", -stacked)
        carry = lax.cond(place >= step, lambda held: absorb(held, upward), lambda held: held, carry)
        carry = lax.cond(
            place + step < group_size, lambda held: absorb(held, downward), lambda held: held, carry
        )
        return (upward, downward, carry)

    final_state = lax.fori_loop(1, group_size, chain_step, (stale_kv, stale_kv, start_carry))
    running_max, running_sum, context = final_state[2]
    attended = jnp.transpose(context / running_sum[..., None], (0, 2, 1, 3)).astype(jnp.bfloat16)
    update = jnp.dot(
        attended.reshape(-1, inner_width), attn_out, preferred_element_type=jnp.float32
    )
    block_out = (widened + update.reshape(images, height, columns, channels)).astype(jnp.bfloat16)
    return (block_out, fresh_kv)


def solution(mesh):
    return jax.shard_map(
        on_device,
        mesh=mesh,
        in_specs=(
            P("img", "band", None, None),
            P("img", "band", None, None),
            P(None, "img", "band", None, None),
            P("img", None),
            P(),
            P(),
            P(),
            P(),
            P(),
            P(),
        ),
        out_specs=(P("img", "band", None, None), P(None, "img", "band", None, None)),
        check_vma=False,
    )
```

profile of v0, /device:TPU:0, one launch (start us, length us, event | category | flops | bytes accessed | tf_op | source)
XLA Modules:
  0.0 1268.4 jit_solution(8291177125210356071)
XLA Ops:
  0.7 2.7 copy.108
  4.1 5.9 collective-permute-start.2
  14.5 351.0 %psum.14 = f32[8,4,32]{2,0,1:T(8,128)S(1)} all-reduce(f32[8,4,32]{2,0,1:T(8,128)S(1)} %broadcast_multiply_fusion.1), channel_id=1, replica_groups=mesh['img'=2,'band'=64] {'band'}, use_global_device_ids=true, to_apply=%region_2.3 | all-reduce | flops 1024 | bytes 8192 | tf_op jit(solution)/shard_map/psum | solution.py:70
  366.5 341.7 %psum.15 = f32[8,4,32]{2,0,1:T(8,128)S(1)} all-reduce(f32[8,4,32]{2,0,1:T(8,128)S(1)} %broadcast_multiply_fusion), channel_id=1, replica_groups=mesh['img'=2,'band'=64] {'band'}, use_global_device_ids=true, to_apply=%region_6.7 | all-reduce | flops 1024 | bytes 8192 | tf_op jit(solution)/shard_map/psum | solution.py:73
  708.5 2.5 copy.90
  713.2 2.8 fusion.47
  718.9 2.6 fusion.49
  731.6 5.4 convolution_convert_fusion
  743.0 3.8 reshape_squeeze_stack.6
  753.3 502.6 %while.21 = (s32[]{:T(128)}, bf16[2,4,4,32,640]{4,3,2,1,0:T(8,128)(2,1)}, bf16[2,4,4,32,640]{4,3,2,1,0:T(8,128)(2,1)}, f32[4,10,128]{2,1,0:T(8,128)S(1)}, f32[4,...) while((s32[]{:T(128)}, ...), condition=%wide.region_21.22_spmd, body=%wide.region_12.21_spmd.sunk | while | flops 348037120 | bytes 72663480 | solution.py:143
  757.0 26.2 %collective-permute-done = bf16[2,4,4,32,640]{4,3,2,1,0:T(8,128)(2,1)} collective-permute-done((bf16[2,4,4,32,640]{4,3,2,1,0:T(8,128)(2,1)}, bf16[2,4,4,32,640]{4,3,2,1,0:T(8,128)(2,1)}, u32[]{:S(2)}, u32[]{:S(2)}) %collective-permute-start) | collective-permute-done | bytes 1310752 | tf_op jit(solution)/shard_map/while/body/eval_jaxpr/ppermute | solution.py:16
  783.2 5.8 collective-permute-done.1
  789.0 17.1 %conditional.5 = ((f32[4,10,128]{2,1,0:T(8,128)S(1)}, f32[4,10,128]{2,1,0:T(8,128)S(1)}, f32[4,10,128,64]{2,3,1,0:T(8,128)S(1)})) conditional(s32[]{:T(128)} %convert_element_type.114, (f32[4,10,128]{2,1,0:T(8,128)S(1)}, f32[4,10,128]{2,1,0:T(8,128)S(1)}, f32[4,10,128,64]{2,3,1,0:T(8,128)S(1)}) %get-tuple-element.368, ...), branch_computations={%region_17.17_spmd, %region_18.20_spmd} | conditional | flops 174018560 | bytes 28467260 | solution.py:138
  791.5 3.5 squeeze.30
  799.4 3.5 squeeze.31
  802.9 3.2 fusion.12
  806.1 2.5 copy.101
  811.1 18.4 %collective-permute-start = (bf16[2,4,4,32,640]{4,3,2,1,0:T(8,128)(2,1)}, bf16[2,4,4,32,640]{4,3,2,1,0:T(8,128)(2,1)}, u32[]{:S(2)}, u32[]{:S(2)}) collective-permute-start(bf16[2,4,4,32,640]{4,3,2,1,0:T(8,128)(2,1)} %get-tuple-element.349), channel_id=1, source_target_pairs={{0,8},{1,9},{2,10},{3,11},{4,12},{5,13},{6,14},{7,15},{8,16},{9,17... | collective-permute-start | bytes 3932168 | tf_op jit(solution)/shard_map/while/body/eval_jaxpr/ppermute | solution.py:16
  830.8 26.5 %collective-permute-done = bf16[2,4,4,32,640]{4,3,2,1,0:T(8,128)(2,1)} collective-permute-done((bf16[2,4,4,32,640]{4,3,2,1,0:T(8,128)(2,1)}, bf16[2,4,4,32,640]{4,3,2,1,0:T(8,128)(2,1)}, u32[]{:S(2)}, u32[]{:S(2)}) %collective-permute-start) | collective-permute-done | bytes 1310752 | tf_op jit(solution)/shard_map/while/body/eval_jaxpr/ppermute | solution.py:16
  857.3 28.8 %collective-permute-done.1 = bf16[2,4,4,32,640]{4,3,2,1,0:T(8,128)(2,1)} collective-permute-done((bf16[2,4,4,32,640]{4,3,2,1,0:T(8,128)(2,1)}, bf16[2,4,4,32,640]{4,3,2,1,0:T(8,128)(2,1)}, u32[]{:S(2)}, u32[]{:S(2)}) %collective-permute-start.1) | collective-permute-done | bytes 1310752 | tf_op jit(solution)/shard_map/while/body/eval_jaxpr/ppermute | solution.py:16
  886.2 17.1 %conditional.5 = ((f32[4,10,128]{2,1,0:T(8,128)S(1)}, f32[4,10,128]{2,1,0:T(8,128)S(1)}, f32[4,10,128,64]{2,3,1,0:T(8,128)S(1)})) conditional(s32[]{:T(128)} %convert_element_type.114, (f32[4,10,128]{2,1,0:T(8,128)S(1)}, f32[4,10,128]{2,1,0:T(8,128)S(1)}, f32[4,10,128,64]{2,3,1,0:T(8,128)S(1)}) %get-tuple-element.368, ...), branch_computations={%region_17.17_spmd, %region_18.20_spmd} | conditional | flops 174018560 | bytes 28467260 | solution.py:138
  888.6 3.5 squeeze.30
  896.5 3.5 squeeze.31
  900.1 3.2 fusion.12
  903.3 2.5 copy.101
  908.3 2.5 collective-permute-start
  912.1 26.1 %collective-permute-done = bf16[2,4,4,32,640]{4,3,2,1,0:T(8,128)(2,1)} collective-permute-done((bf16[2,4,4,32,640]{4,3,2,1,0:T(8,128)(2,1)}, bf16[2,4,4,32,640]{4,3,2,1,0:T(8,128)(2,1)}, u32[]{:S(2)}, u32[]{:S(2)}) %collective-permute-start) | collective-permute-done | bytes 1310752 | tf_op jit(solution)/shard_map/while/body/eval_jaxpr/ppermute | solution.py:16
  938.2 28.7 %collective-permute-done.1 = bf16[2,4,4,32,640]{4,3,2,1,0:T(8,128)(2,1)} collective-permute-done((bf16[2,4,4,32,640]{4,3,2,1,0:T(8,128)(2,1)}, bf16[2,4,4,32,640]{4,3,2,1,0:T(8,128)(2,1)}, u32[]{:S(2)}, u32[]{:S(2)}) %collective-permute-start.1) | collective-permute-done | bytes 1310752 | tf_op jit(solution)/shard_map/while/body/eval_jaxpr/ppermute | solution.py:16
  966.9 17.1 %conditional.5 = ((f32[4,10,128]{2,1,0:T(8,128)S(1)}, f32[4,10,128]{2,1,0:T(8,128)S(1)}, f32[4,10,128,64]{2,3,1,0:T(8,128)S(1)})) conditional(s32[]{:T(128)} %convert_element_type.114, (f32[4,10,128]{2,1,0:T(8,128)S(1)}, f32[4,10,128]{2,1,0:T(8,128)S(1)}, f32[4,10,128,64]{2,3,1,0:T(8,128)S(1)}) %get-tuple-element.368, ...), branch_computations={%region_17.17_spmd, %region_18.20_spmd} | conditional | flops 174018560 | bytes 28467260 | solution.py:138
  969.4 3.5 squeeze.30
  977.3 3.5 squeeze.31
  980.8 3.2 fusion.12
  984.0 2.5 copy.101
  989.0 2.6 collective-permute-start
  992.9 25.5 %collective-permute-done = bf16[2,4,4,32,640]{4,3,2,1,0:T(8,128)(2,1)} collective-permute-done((bf16[2,4,4,32,640]{4,3,2,1,0:T(8,128)(2,1)}, bf16[2,4,4,32,640]{4,3,2,1,0:T(8,128)(2,1)}, u32[]{:S(2)}, u32[]{:S(2)}) %collective-permute-start) | collective-permute-done | bytes 1310752 | tf_op jit(solution)/shard_map/while/body/eval_jaxpr/ppermute | solution.py:16
  1018.4 28.7 %collective-permute-done.1 = bf16[2,4,4,32,640]{4,3,2,1,0:T(8,128)(2,1)} collective-permute-done((bf16[2,4,4,32,640]{4,3,2,1,0:T(8,128)(2,1)}, bf16[2,4,4,32,640]{4,3,2,1,0:T(8,128)(2,1)}, u32[]{:S(2)}, u32[]{:S(2)}) %collective-permute-start.1) | collective-permute-done | bytes 1310752 | tf_op jit(solution)/shard_map/while/body/eval_jaxpr/ppermute | solution.py:16
  1047.1 17.1 %conditional.5 = ((f32[4,10,128]{2,1,0:T(8,128)S(1)}, f32[4,10,128]{2,1,0:T(8,128)S(1)}, f32[4,10,128,64]{2,3,1,0:T(8,128)S(1)})) conditional(s32[]{:T(128)} %convert_element_type.114, (f32[4,10,128]{2,1,0:T(8,128)S(1)}, f32[4,10,128]{2,1,0:T(8,128)S(1)}, f32[4,10,128,64]{2,3,1,0:T(8,128)S(1)}) %get-tuple-element.368, ...), branch_computations={%region_17.17_spmd, %region_18.20_spmd} | conditional | flops 174018560 | bytes 28467260 | solution.py:138
  1049.6 3.5 squeeze.30
  1057.5 3.5 squeeze.31
  1061.0 3.2 fusion.12
  1064.2 2.5 copy.101
  1069.3 2.6 collective-permute-start
  1073.1 24.9 %collective-permute-done = bf16[2,4,4,32,640]{4,3,2,1,0:T(8,128)(2,1)} collective-permute-done((bf16[2,4,4,32,640]{4,3,2,1,0:T(8,128)(2,1)}, bf16[2,4,4,32,640]{4,3,2,1,0:T(8,128)(2,1)}, u32[]{:S(2)}, u32[]{:S(2)}) %collective-permute-start) | collective-permute-done | bytes 1310752 | tf_op jit(solution)/shard_map/while/body/eval_jaxpr/ppermute | solution.py:16
  1098.0 28.7 %collective-permute-done.1 = bf16[2,4,4,32,640]{4,3,2,1,0:T(8,128)(2,1)} collective-permute-done((bf16[2,4,4,32,640]{4,3,2,1,0:T(8,128)(2,1)}, bf16[2,4,4,32,640]{4,3,2,1,0:T(8,128)(2,1)}, u32[]{:S(2)}, u32[]{:S(2)}) %collective-permute-start.1) | collective-permute-done | bytes 1310752 | tf_op jit(solution)/shard_map/while/body/eval_jaxpr/ppermute | solution.py:16
  1126.7 17.1 %conditional.5 = ((f32[4,10,128]{2,1,0:T(8,128)S(1)}, f32[4,10,128]{2,1,0:T(8,128)S(1)}, f32[4,10,128,64]{2,3,1,0:T(8,128)S(1)})) conditional(s32[]{:T(128)} %convert_element_type.114, (f32[4,10,128]{2,1,0:T(8,128)S(1)}, f32[4,10,128]{2,1,0:T(8,128)S(1)}, f32[4,10,128,64]{2,3,1,0:T(8,128)S(1)}) %get-tuple-element.368, ...), branch_computations={%region_17.17_spmd, %region_18.20_spmd} | conditional | flops 174018560 | bytes 28467260 | solution.py:138
  1129.2 3.5 squeeze.30
  1137.1 3.5 squeeze.31
  1140.6 3.2 fusion.12
  1148.9 2.5 collective-permute-start
  1152.7 13.0 %collective-permute-done = bf16[2,4,4,32,640]{4,3,2,1,0:T(8,128)(2,1)} collective-permute-done((bf16[2,4,4,32,640]{4,3,2,1,0:T(8,128)(2,1)}, bf16[2,4,4,32,640]{4,3,2,1,0:T(8,128)(2,1)}, u32[]{:S(2)}, u32[]{:S(2)}) %collective-permute-start) | collective-permute-done | bytes 1310752 | tf_op jit(solution)/shard_map/while/body/eval_jaxpr/ppermute | solution.py:16
  1165.7 14.5 %collective-permute-done.1 = bf16[2,4,4,32,640]{4,3,2,1,0:T(8,128)(2,1)} collective-permute-done((bf16[2,4,4,32,640]{4,3,2,1,0:T(8,128)(2,1)}, bf16[2,4,4,32,640]{4,3,2,1,0:T(8,128)(2,1)}, u32[]{:S(2)}, u32[]{:S(2)}) %collective-permute-start.1) | collective-permute-done | bytes 1310752 | tf_op jit(solution)/shard_map/while/body/eval_jaxpr/ppermute | solution.py:16
  1180.2 17.1 %conditional.5 = ((f32[4,10,128]{2,1,0:T(8,128)S(1)}, f32[4,10,128]{2,1,0:T(8,128)S(1)}, f32[4,10,128,64]{2,3,1,0:T(8,128)S(1)})) conditional(s32[]{:T(128)} %convert_element_type.114, (f32[4,10,128]{2,1,0:T(8,128)S(1)}, f32[4,10,128]{2,1,0:T(8,128)S(1)}, f32[4,10,128,64]{2,3,1,0:T(8,128)S(1)}) %get-tuple-element.368, ...), branch_computations={%region_17.17_spmd, %region_18.20_spmd} | conditional | flops 174018560 | bytes 28467260 | solution.py:138
  1182.7 3.5 squeeze.30
  1190.6 3.5 squeeze.31
  1194.1 3.2 fusion.12
  1202.4 2.6 collective-permute-start
  1206.2 13.0 %collective-permute-done = bf16[2,4,4,32,640]{4,3,2,1,0:T(8,128)(2,1)} collective-permute-done((bf16[2,4,4,32,640]{4,3,2,1,0:T(8,128)(2,1)}, bf16[2,4,4,32,640]{4,3,2,1,0:T(8,128)(2,1)}, u32[]{:S(2)}, u32[]{:S(2)}) %collective-permute-start) | collective-permute-done | bytes 1310752 | tf_op jit(solution)/shard_map/while/body/eval_jaxpr/ppermute | solution.py:16
  1219.2 14.5 %collective-permute-done.1 = bf16[2,4,4,32,640]{4,3,2,1,0:T(8,128)(2,1)} collective-permute-done((bf16[2,4,4,32,640]{4,3,2,1,0:T(8,128)(2,1)}, bf16[2,4,4,32,640]{4,3,2,1,0:T(8,128)(2,1)}, u32[]{:S(2)}, u32[]{:S(2)}) %collective-permute-start.1) | collective-permute-done | bytes 1310752 | tf_op jit(solution)/shard_map/while/body/eval_jaxpr/ppermute | solution.py:16
  1233.7 17.1 %conditional.5 = ((f32[4,10,128]{2,1,0:T(8,128)S(1)}, f32[4,10,128]{2,1,0:T(8,128)S(1)}, f32[4,10,128,64]{2,3,1,0:T(8,128)S(1)})) conditional(s32[]{:T(128)} %convert_element_type.114, (f32[4,10,128]{2,1,0:T(8,128)S(1)}, f32[4,10,128]{2,1,0:T(8,128)S(1)}, f32[4,10,128,64]{2,3,1,0:T(8,128)S(1)}) %get-tuple-element.368, ...), branch_computations={%region_17.17_spmd, %region_18.20_spmd} | conditional | flops 174018560 | bytes 28467260 | solution.py:138
  1236.2 3.5 squeeze.30
  1244.1 3.5 squeeze.31
  1247.6 3.2 fusion.12
  1256.9 3.4 copy.44
  1260.3 3.8 dot_general.69
  (157 shorter events, 123.1 us)
Async XLA Ops:
  0.6 1264.7 %copy-start = (bf16[640,1280]{1,0:T(8,128)(2,1)S(1)}, bf16[640,1280]{1,0:T(8,128)(2,1)}, u32[]{:S(2)}) copy-start(bf16[640,1280]{1,0:T(8,128)(2,1)} %param.25) | copy-start | bytes 4915204
  0.6 10.7 copy-start.4
  0.7 2.7 copy-start.16
  4.1 711.9 %collective-permute-start.2 = (bf16[4,1,32,1280]{3,2,1,0:T(8,128)(2,1)}, bf16[4,1,32,1280]{3,2,1,0:T(8,128)(2,1)}, u32[]{:S(2)}, u32[]{:S(2)}) collective-permute-start(bf16[4,1,32,1280]{3,2,1,0:T(8,128)(2,1)} %get-tuple-element.259), channel_id=1, source_target_pairs={{0,8},{1,9},{2,10},{3,11},{4,12},{5,13},{6,14},{7,15},{8,16},{9,17... | collective-permute-start | bytes 983048 | tf_op jit(solution)/shard_map/ppermute | solution.py:16
  10.0 706.0 %collective-permute-start.3 = (bf16[4,1,32,1280]{3,2,1,0:T(8,128)(2,1)S(1)}, bf16[4,1,32,1280]{3,2,1,0:T(8,128)(2,1)}, u32[]{:S(2)}, u32[]{:S(2)}) collective-permute-start(bf16[4,1,32,1280]{3,2,1,0:T(8,128)(2,1)S(1)} %get-tuple-element.260), channel_id=1, source_target_pairs={{8,0},{9,1},{10,2},{11,3},{12,4},{13,5},{14,6},{15,7},{16,8},{17,9... | collective-permute-start | bytes 983048 | tf_op jit(solution)/shard_map/ppermute | solution.py:16
  365.8 345.2 %copy-start.19 = (s32[4,8]{1,0:T(4,128)S(1)}, s32[4,8]{1,0:T(4,128)}, u32[]{:S(2)}) copy-start(s32[4,8]{1,0:T(4,128)} %param.19) | copy-start | bytes 388
  365.8 345.5 %copy-start.17 = (f32[1280]{0:T(1024)S(1)}, f32[1280]{0:T(1024)}, u32[]{:S(2)}) copy-start(f32[1280]{0:T(1024)} %param.21) | copy-start | bytes 15364
  365.9 345.5 %copy-start.18 = (f32[1280]{0:T(1024)S(1)}, f32[1280]{0:T(1024)}, u32[]{:S(2)}) copy-start(f32[1280]{0:T(1024)} %param.20) | copy-start | bytes 15364
  711.0 1.4 copy-start.13
  713.2 8.4 copy-start.14
  727.6 1.7 copy-start.9
  729.3 1.3 copy-start.7
  730.6 6.4 copy-start.5
  743.0 5.9 copy-start.3
  751.0 1.6 copy-start.10
  753.3 29.9 %collective-permute-start = (bf16[2,4,4,32,640]{4,3,2,1,0:T(8,128)(2,1)}, bf16[2,4,4,32,640]{4,3,2,1,0:T(8,128)(2,1)}, u32[]{:S(2)}, u32[]{:S(2)}) collective-permute-start(bf16[2,4,4,32,640]{4,3,2,1,0:T(8,128)(2,1)} %get-tuple-element.349), channel_id=1, source_target_pairs={{0,8},{1,9},{2,10},{3,11},{4,12},{5,13},{6,14},{7,15},{8,16},{9,17... | collective-permute-start | bytes 3932168 | tf_op jit(solution)/shard_map/while/body/eval_jaxpr/ppermute | solution.py:16
  755.7 33.3 %collective-permute-start.1 = (bf16[2,4,4,32,640]{4,3,2,1,0:T(8,128)(2,1)}, bf16[2,4,4,32,640]{4,3,2,1,0:T(8,128)(2,1)}, u32[]{:S(2)}, u32[]{:S(2)}) collective-permute-start(bf16[2,4,4,32,640]{4,3,2,1,0:T(8,128)(2,1)} %get-tuple-element.350), channel_id=1, source_target_pairs={{8,0},{9,1},{10,2},{11,3},{12,4},{13,5},{14,6},{15,7},{16,8},{17,9... | collective-permute-start | bytes 3932168 | tf_op jit(solution)/shard_map/while/body/eval_jaxpr/ppermute | solution.py:16
  797.3 1.5 copy-start.2
  811.1 46.2 %collective-permute-start = (bf16[2,4,4,32,640]{4,3,2,1,0:T(8,128)(2,1)}, bf16[2,4,4,32,640]{4,3,2,1,0:T(8,128)(2,1)}, u32[]{:S(2)}, u32[]{:S(2)}) collective-permute-start(bf16[2,4,4,32,640]{4,3,2,1,0:T(8,128)(2,1)} %get-tuple-element.349), channel_id=1, source_target_pairs={{0,8},{1,9},{2,10},{3,11},{4,12},{5,13},{6,14},{7,15},{8,16},{9,17... | collective-permute-start | bytes 3932168 | tf_op jit(solution)/shard_map/while/body/eval_jaxpr/ppermute | solution.py:16
  829.5 56.7 %collective-permute-start.1 = (bf16[2,4,4,32,640]{4,3,2,1,0:T(8,128)(2,1)}, bf16[2,4,4,32,640]{4,3,2,1,0:T(8,128)(2,1)}, u32[]{:S(2)}, u32[]{:S(2)}) collective-permute-start(bf16[2,4,4,32,640]{4,3,2,1,0:T(8,128)(2,1)} %get-tuple-element.350), channel_id=1, source_target_pairs={{8,0},{9,1},{10,2},{11,3},{12,4},{13,5},{14,6},{15,7},{16,8},{17,9... | collective-permute-start | bytes 3932168 | tf_op jit(solution)/shard_map/while/body/eval_jaxpr/ppermute | solution.py:16
  894.4 1.5 copy-start.2
  908.3 29.9 %collective-permute-start = (bf16[2,4,4,32,640]{4,3,2,1,0:T(8,128)(2,1)}, bf16[2,4,4,32,640]{4,3,2,1,0:T(8,128)(2,1)}, u32[]{:S(2)}, u32[]{:S(2)}) collective-permute-start(bf16[2,4,4,32,640]{4,3,2,1,0:T(8,128)(2,1)} %get-tuple-element.349), channel_id=1, source_target_pairs={{0,8},{1,9},{2,10},{3,11},{4,12},{5,13},{6,14},{7,15},{8,16},{9,17... | collective-permute-start | bytes 3932168 | tf_op jit(solution)/shard_map/while/body/eval_jaxpr/ppermute | solution.py:16
  910.8 56.1 %collective-permute-start.1 = (bf16[2,4,4,32,640]{4,3,2,1,0:T(8,128)(2,1)}, bf16[2,4,4,32,640]{4,3,2,1,0:T(8,128)(2,1)}, u32[]{:S(2)}, u32[]{:S(2)}) collective-permute-start(bf16[2,4,4,32,640]{4,3,2,1,0:T(8,128)(2,1)} %get-tuple-element.350), channel_id=1, source_target_pairs={{8,0},{9,1},{10,2},{11,3},{12,4},{13,5},{14,6},{15,7},{16,8},{17,9... | collective-permute-start | bytes 3932168 | tf_op jit(solution)/shard_map/while/body/eval_jaxpr/ppermute | solution.py:16
  975.2 1.5 copy-start.2
  989.0 29.4 %collective-permute-start = (bf16[2,4,4,32,640]{4,3,2,1,0:T(8,128)(2,1)}, bf16[2,4,4,32,640]{4,3,2,1,0:T(8,128)(2,1)}, u32[]{:S(2)}, u32[]{:S(2)}) collective-permute-start(bf16[2,4,4,32,640]{4,3,2,1,0:T(8,128)(2,1)} %get-tuple-element.349), channel_id=1, source_target_pairs={{0,8},{1,9},{2,10},{3,11},{4,12},{5,13},{6,14},{7,15},{8,16},{9,17... | collective-permute-start | bytes 3932168 | tf_op jit(solution)/shard_map/while/body/eval_jaxpr/ppermute | solution.py:16
  991.6 55.5 %collective-permute-start.1 = (bf16[2,4,4,32,640]{4,3,2,1,0:T(8,128)(2,1)}, bf16[2,4,4,32,640]{4,3,2,1,0:T(8,128)(2,1)}, u32[]{:S(2)}, u32[]{:S(2)}) collective-permute-start(bf16[2,4,4,32,640]{4,3,2,1,0:T(8,128)(2,1)} %get-tuple-element.350), channel_id=1, source_target_pairs={{8,0},{9,1},{10,2},{11,3},{12,4},{13,5},{14,6},{15,7},{16,8},{17,9... | collective-permute-start | bytes 3932168 | tf_op jit(solution)/shard_map/while/body/eval_jaxpr/ppermute | solution.py:16
  1055.4 1.5 copy-start.2
  1069.3 28.7 %collective-permute-start = (bf16[2,4,4,32,640]{4,3,2,1,0:T(8,128)(2,1)}, bf16[2,4,4,32,640]{4,3,2,1,0:T(8,128)(2,1)}, u32[]{:S(2)}, u32[]{:S(2)}) collective-permute-start(bf16[2,4,4,32,640]{4,3,2,1,0:T(8,128)(2,1)} %get-tuple-element.349), channel_id=1, source_target_pairs={{0,8},{1,9},{2,10},{3,11},{4,12},{5,13},{6,14},{7,15},{8,16},{9,17... | collective-permute-start | bytes 3932168 | tf_op jit(solution)/shard_map/while/body/eval_jaxpr/ppermute | solution.py:16
  1071.8 54.9 %collective-permute-start.1 = (bf16[2,4,4,32,640]{4,3,2,1,0:T(8,128)(2,1)}, bf16[2,4,4,32,640]{4,3,2,1,0:T(8,128)(2,1)}, u32[]{:S(2)}, u32[]{:S(2)}) collective-permute-start(bf16[2,4,4,32,640]{4,3,2,1,0:T(8,128)(2,1)} %get-tuple-element.350), channel_id=1, source_target_pairs={{8,0},{9,1},{10,2},{11,3},{12,4},{13,5},{14,6},{15,7},{16,8},{17,9... | collective-permute-start | bytes 3932168 | tf_op jit(solution)/shard_map/while/body/eval_jaxpr/ppermute | solution.py:16
  1135.0 1.5 copy-start.2
  1148.9 16.9 %collective-permute-start = (bf16[2,4,4,32,640]{4,3,2,1,0:T(8,128)(2,1)}, bf16[2,4,4,32,640]{4,3,2,1,0:T(8,128)(2,1)}, u32[]{:S(2)}, u32[]{:S(2)}) collective-permute-start(bf16[2,4,4,32,640]{4,3,2,1,0:T(8,128)(2,1)} %get-tuple-element.349), channel_id=1, source_target_pairs={{0,8},{1,9},{2,10},{3,11},{4,12},{5,13},{6,14},{7,15},{8,16},{9,17... | collective-permute-start | bytes 3932168 | tf_op jit(solution)/shard_map/while/body/eval_jaxpr/ppermute | solution.py:16
  1151.4 28.8 %collective-permute-start.1 = (bf16[2,4,4,32,640]{4,3,2,1,0:T(8,128)(2,1)}, bf16[2,4,4,32,640]{4,3,2,1,0:T(8,128)(2,1)}, u32[]{:S(2)}, u32[]{:S(2)}) collective-permute-start(bf16[2,4,4,32,640]{4,3,2,1,0:T(8,128)(2,1)} %get-tuple-element.350), channel_id=1, source_target_pairs={{8,0},{9,1},{10,2},{11,3},{12,4},{13,5},{14,6},{15,7},{16,8},{17,9... | collective-permute-start | bytes 3932168 | tf_op jit(solution)/shard_map/while/body/eval_jaxpr/ppermute | solution.py:16
  1188.5 1.5 copy-start.2
  1202.4 16.9 %collective-permute-start = (bf16[2,4,4,32,640]{4,3,2,1,0:T(8,128)(2,1)}, bf16[2,4,4,32,640]{4,3,2,1,0:T(8,128)(2,1)}, u32[]{:S(2)}, u32[]{:S(2)}) collective-permute-start(bf16[2,4,4,32,640]{4,3,2,1,0:T(8,128)(2,1)} %get-tuple-element.349), channel_id=1, source_target_pairs={{0,8},{1,9},{2,10},{3,11},{4,12},{5,13},{6,14},{7,15},{8,16},{9,17... | collective-permute-start | bytes 3932168 | tf_op jit(solution)/shard_map/while/body/eval_jaxpr/ppermute | solution.py:16
  1204.9 28.8 %collective-permute-start.1 = (bf16[2,4,4,32,640]{4,3,2,1,0:T(8,128)(2,1)}, bf16[2,4,4,32,640]{4,3,2,1,0:T(8,128)(2,1)}, u32[]{:S(2)}, u32[]{:S(2)}) collective-permute-start(bf16[2,4,4,32,640]{4,3,2,1,0:T(8,128)(2,1)} %get-tuple-element.350), channel_id=1, source_target_pairs={{8,0},{9,1},{10,2},{11,3},{12,4},{13,5},{14,6},{15,7},{16,8},{17,9... | collective-permute-start | bytes 3932168 | tf_op jit(solution)/shard_map/while/body/eval_jaxpr/ppermute | solution.py:16
  1242.0 1.5 copy-start.2
  1260.3 3.8 copy-start.11
  1260.3 3.8 copy-start.12
  1264.1 1.2 copy-start.6
  1264.1 1.8 copy-start.8
  1264.1 2.0 copy-start.15
where the time goes:
time: 1270 us
  blocking collectives  693 us (55%)
  waiting for transfers between devices  305 us (24%)
  local copies, waits for them, and re-layouts  141 us (11%)
  matrix products  63.4 us (5%)
  starting transfers between devices  49.7 us (4%)
  other arithmetic  14.6 us (1%)
    psum x1, blocking collectives, on_device(): totals = lax.psum(slot_mask * jnp.sum(grouped, axis=(1, 3))[None], 'band')  351 us
    psum x1, blocking collectives, on_device(): lax.psum(slot_mask * jnp.sum(deviation * deviation, axis=(1, 3))[None], '...  342 us
    ppermute x16, waiting for transfers between devices, shifted(): return lax.ppermute(value, axis, pairs)  305 us
    ppermute x16, starting transfers between devices, shifted(): return lax.ppermute(value, axis, pairs)  49.7 us
    while x14, local copies, waits for them, and re-layouts  35.1 us
  transfers between devices with their start and end apart: 16, of which 14 were waited for; matrix products, arithmetic and copies ran while one was open for 1% of the time, Pallas kernels for 0%

commit v1 on v0

--- a/solution.py
+++ b/solution.py
@@ -70,7 +70,9 @@
     totals = lax.psum(slot_mask * jnp.sum(grouped, axis=(1, 3))[None], "band")
     center = jnp.sum(totals * slot_mask, axis=0) / counted
     deviation = grouped - center[:, None, :, None]
-    spreads = lax.psum(slot_mask * jnp.sum(deviation * deviation, axis=(1, 3))[None], "band")
+    x = slot_mask * jnp.sum(deviation * deviation, axis=(1, 3))[None]
+    parts = lax.all_gather(x, "band")
+    spreads = jnp.sum(parts, axis=0)
     spread = jnp.sum(spreads * slot_mask, axis=0) / counted
     normed = (
         (grouped - center[:, None, :, None]) / jnp.sqrt(spread + 1e-05)[:, None, :, None]

time: 1270 us -> 1090 us (0.86)
  blocking collectives: 693 us -> 536 us
  waiting for transfers between devices: 305 us -> 263 us
    psum x1 -> x0, blocking collectives: 342 us -> none  [on_device(): lax.psum(slot_mask * jnp.sum(deviation * deviation, axis=(1, 3))[None], '...]
    all_gather x0 -> x1, blocking collectives: none -> 185 us  [on_device(): parts = lax.all_gather(x, 'band')]
    ppermute x16, waiting for transfers between devices: 305 us -> 263 us  [shifted(): return lax.ppermute(value, axis, pairs)]
where the time goes in v1:
time: 1090 us; the launch traced here: 1080 us
  blocking collectives  536 us (49%)
  waiting for transfers between devices  263 us (24%)
  local copies, waits for them, and re-layouts  141 us (13%)
  matrix products  63.4 us (6%)
  starting transfers between devices  54.6 us (5%)
  other arithmetic  16 us (1%)
    psum x1, blocking collectives, on_device(): totals = lax.psum(slot_mask * jnp.sum(grouped, axis=(1, 3))[None], 'band')  351 us
    ppermute x16, waiting for transfers between devices, shifted(): return lax.ppermute(value, axis, pairs)  263 us
    all_gather x1, blocking collectives, on_device(): parts = lax.all_gather(x, 'band')  185 us
    ppermute x16, starting transfers between devices, shifted(): return lax.ppermute(value, axis, pairs)  54.6 us
    while x14, local copies, waits for them, and re-layouts  35.1 us
    squeeze x7, local copies, waits for them, and re-layouts, absorb(): piece[0].reshape(images, piece_rows * columns, head_count, head_size)  24.8 us
    squeeze x7, local copies, waits for them, and re-layouts, absorb(): piece[1].reshape(images, piece_rows * columns, head_count, head_size)  24.8 us
    dot_general x8, matrix products, attend_block(): jnp.einsum('bhqk,bkhd->bhqd', exponent.astype(jnp.bfloat16), values, pref...  23.1 us
  transfers between devices with their start and end apart: 16, of which 14 were waited for; matrix products, arithmetic and copies ran while one was open for 1% of the time, Pallas kernels for 0%

profile of v1, /device:TPU:0, one launch (start us, length us, event | category | flops | bytes accessed | tf_op | source)
XLA Modules:
  0.0 1075.8 jit_solution(10062161369199987397)
XLA Ops:
  0.7 2.7 copy.132
  4.1 5.9 collective-permute-start.2
  14.5 351.0 %psum.7 = f32[8,4,32]{2,0,1:T(8,128)S(1)} all-reduce(f32[8,4,32]{2,0,1:T(8,128)S(1)} %broadcast_multiply_fusion.1), channel_id=1, replica_groups=mesh['img'=2,'band'=64] {'band'}, use_global_device_ids=true, to_apply=%region_2.3 | all-reduce | flops 1024 | bytes 8192 | tf_op jit(solution)/shard_map/psum | solution.py:70
  366.5 185.2 %all_gather.4 = f32[64,8,4,32]{3,1,2,0:T(8,128)} all-gather(f32[1,8,4,32]{3,1,2,0:T(8,128)S(1)} %broadcast_multiply_fusion), channel_id=1, replica_groups=mesh['img'=2,'band'=64] {'band'}, dimensions={0}, use_global_device_ids=true | all-gather | bytes 266240 | tf_op jit(solution)/shard_map/all_gather | solution.py:74
  553.4 2.5 copy.114
  558.1 2.8 fusion.47
  563.8 2.6 fusion.49
  576.4 5.4 convolution_convert_fusion
  587.9 3.8 reshape_squeeze_stack.6
  598.2 465.2 %while.21 = (s32[]{:T(128)}, bf16[2,4,4,32,640]{4,3,2,1,0:T(8,128)(2,1)}, bf16[2,4,4,32,640]{4,3,2,1,0:T(8,128)(2,1)}, f32[4,10,128]{2,1,0:T(8,128)S(1)}, f32[4,...) while((s32[]{:T(128)}, ...), condition=%wide.region_21.22_spmd, body=%wide.region_12.21_spmd.sunk | while | flops 348037120 | bytes 72663480 | solution.py:145
  601.9 13.0 %collective-permute-done = bf16[2,4,4,32,640]{4,3,2,1,0:T(8,128)(2,1)} collective-permute-done((bf16[2,4,4,32,640]{4,3,2,1,0:T(8,128)(2,1)}, bf16[2,4,4,32,640]{4,3,2,1,0:T(8,128)(2,1)}, u32[]{:S(2)}, u32[]{:S(2)}) %collective-permute-start) | collective-permute-done | bytes 1310752 | tf_op jit(solution)/shard_map/while/body/eval_jaxpr/ppermute | solution.py:16
  614.9 19.3 %collective-permute-done.1 = bf16[2,4,4,32,640]{4,3,2,1,0:T(8,128)(2,1)} collective-permute-done((bf16[2,4,4,32,640]{4,3,2,1,0:T(8,128)(2,1)}, bf16[2,4,4,32,640]{4,3,2,1,0:T(8,128)(2,1)}, u32[]{:S(2)}, u32[]{:S(2)}) %collective-permute-start.1) | collective-permute-done | bytes 1310752 | tf_op jit(solution)/shard_map/while/body/eval_jaxpr/ppermute | solution.py:16
  634.2 17.1 %conditional.5 = ((f32[4,10,128]{2,1,0:T(8,128)S(1)}, f32[4,10,128]{2,1,0:T(8,128)S(1)}, f32[4,10,128,64]{2,3,1,0:T(8,128)S(1)})) conditional(s32[]{:T(128)} %convert_element_type.114, (f32[4,10,128]{2,1,0:T(8,128)S(1)}, f32[4,10,128]{2,1,0:T(8,128)S(1)}, f32[4,10,128,64]{2,3,1,0:T(8,128)S(1)}) %get-tuple-element.384, ...), branch_computations={%region_17.17_spmd, %region_18.20_spmd} | conditional | flops 174018560 | bytes 28467260 | solution.py:140
  636.7 3.5 squeeze.30
  644.6 3.5 squeeze.31
  648.1 3.2 fusion.12
  651.3 2.5 copy.125
  656.3 4.8 collective-permute-start
  662.4 16.6 %collective-permute-done = bf16[2,4,4,32,640]{4,3,2,1,0:T(8,128)(2,1)} collective-permute-done((bf16[2,4,4,32,640]{4,3,2,1,0:T(8,128)(2,1)}, bf16[2,4,4,32,640]{4,3,2,1,0:T(8,128)(2,1)}, u32[]{:S(2)}, u32[]{:S(2)}) %collective-permute-start) | collective-permute-done | bytes 1310752 | tf_op jit(solution)/shard_map/while/body/eval_jaxpr/ppermute | solution.py:16
  679.0 28.7 %collective-permute-done.1 = bf16[2,4,4,32,640]{4,3,2,1,0:T(8,128)(2,1)} collective-permute-done((bf16[2,4,4,32,640]{4,3,2,1,0:T(8,128)(2,1)}, bf16[2,4,4,32,640]{4,3,2,1,0:T(8,128)(2,1)}, u32[]{:S(2)}, u32[]{:S(2)}) %collective-permute-start.1) | collective-permute-done | bytes 1310752 | tf_op jit(solution)/shard_map/while/body/eval_jaxpr/ppermute | solution.py:16
  707.7 17.1 %conditional.5 = ((f32[4,10,128]{2,1,0:T(8,128)S(1)}, f32[4,10,128]{2,1,0:T(8,128)S(1)}, f32[4,10,128,64]{2,3,1,0:T(8,128)S(1)})) conditional(s32[]{:T(128)} %convert_element_type.114, (f32[4,10,128]{2,1,0:T(8,128)S(1)}, f32[4,10,128]{2,1,0:T(8,128)S(1)}, f32[4,10,128,64]{2,3,1,0:T(8,128)S(1)}) %get-tuple-element.384, ...), branch_computations={%region_17.17_spmd, %region_18.20_spmd} | conditional | flops 174018560 | bytes 28467260 | solution.py:140
  710.2 3.5 squeeze.30
  718.1 3.5 squeeze.31
  721.6 3.2 fusion.12
  724.8 2.5 copy.125
  729.9 2.6 collective-permute-start
  733.7 15.9 %collective-permute-done = bf16[2,4,4,32,640]{4,3,2,1,0:T(8,128)(2,1)} collective-permute-done((bf16[2,4,4,32,640]{4,3,2,1,0:T(8,128)(2,1)}, bf16[2,4,4,32,640]{4,3,2,1,0:T(8,128)(2,1)}, u32[]{:S(2)}, u32[]{:S(2)}) %collective-permute-start) | collective-permute-done | bytes 1310752 | tf_op jit(solution)/shard_map/while/body/eval_jaxpr/ppermute | solution.py:16
  749.7 28.7 %collective-permute-done.1 = bf16[2,4,4,32,640]{4,3,2,1,0:T(8,128)(2,1)} collective-permute-done((bf16[2,4,4,32,640]{4,3,2,1,0:T(8,128)(2,1)}, bf16[2,4,4,32,640]{4,3,2,1,0:T(8,128)(2,1)}, u32[]{:S(2)}, u32[]{:S(2)}) %collective-permute-start.1) | collective-permute-done | bytes 1310752 | tf_op jit(solution)/shard_map/while/body/eval_jaxpr/ppermute | solution.py:16
  778.4 17.1 %conditional.5 = ((f32[4,10,128]{2,1,0:T(8,128)S(1)}, f32[4,10,128]{2,1,0:T(8,128)S(1)}, f32[4,10,128,64]{2,3,1,0:T(8,128)S(1)})) conditional(s32[]{:T(128)} %convert_element_type.114, (f32[4,10,128]{2,1,0:T(8,128)S(1)}, f32[4,10,128]{2,1,0:T(8,128)S(1)}, f32[4,10,128,64]{2,3,1,0:T(8,128)S(1)}) %get-tuple-element.384, ...), branch_computations={%region_17.17_spmd, %region_18.20_spmd} | conditional | flops 174018560 | bytes 28467260 | solution.py:140
  780.8 3.5 squeeze.30
  788.7 3.5 squeeze.31
  792.2 3.2 fusion.12
  795.5 2.5 copy.125
  800.5 2.6 collective-permute-start
  804.3 13.0 %collective-permute-done = bf16[2,4,4,32,640]{4,3,2,1,0:T(8,128)(2,1)} collective-permute-done((bf16[2,4,4,32,640]{4,3,2,1,0:T(8,128)(2,1)}, bf16[2,4,4,32,640]{4,3,2,1,0:T(8,128)(2,1)}, u32[]{:S(2)}, u32[]{:S(2)}) %collective-permute-start) | collective-permute-done | bytes 1310752 | tf_op jit(solution)/shard_map/while/body/eval_jaxpr/ppermute | solution.py:16
  817.4 26.6 %collective-permute-done.1 = bf16[2,4,4,32,640]{4,3,2,1,0:T(8,128)(2,1)} collective-permute-done((bf16[2,4,4,32,640]{4,3,2,1,0:T(8,128)(2,1)}, bf16[2,4,4,32,640]{4,3,2,1,0:T(8,128)(2,1)}, u32[]{:S(2)}, u32[]{:S(2)}) %collective-permute-start.1) | collective-permute-done | bytes 1310752 | tf_op jit(solution)/shard_map/while/body/eval_jaxpr/ppermute | solution.py:16
  844.0 17.1 %conditional.5 = ((f32[4,10,128]{2,1,0:T(8,128)S(1)}, f32[4,10,128]{2,1,0:T(8,128)S(1)}, f32[4,10,128,64]{2,3,1,0:T(8,128)S(1)})) conditional(s32[]{:T(128)} %convert_element_type.114, (f32[4,10,128]{2,1,0:T(8,128)S(1)}, f32[4,10,128]{2,1,0:T(8,128)S(1)}, f32[4,10,128,64]{2,3,1,0:T(8,128)S(1)}) %get-tuple-element.384, ...), branch_computations={%region_17.17_spmd, %region_18.20_spmd} | conditional | flops 174018560 | bytes 28467260 | solution.py:140
  846.5 3.5 squeeze.30
  854.3 3.5 squeeze.31
  857.9 3.2 fusion.12
  861.1 2.5 copy.125
  866.1 2.6 collective-permute-start
  870.0 13.0 %collective-permute-done = bf16[2,4,4,32,640]{4,3,2,1,0:T(8,128)(2,1)} collective-permute-done((bf16[2,4,4,32,640]{4,3,2,1,0:T(8,128)(2,1)}, bf16[2,4,4,32,640]{4,3,2,1,0:T(8,128)(2,1)}, u32[]{:S(2)}, u32[]{:S(2)}) %collective-permute-start) | collective-permute-done | bytes 1310752 | tf_op jit(solution)/shard_map/while/body/eval_jaxpr/ppermute | solution.py:16
  883.0 32.7 %collective-permute-done.1 = bf16[2,4,4,32,640]{4,3,2,1,0:T(8,128)(2,1)} collective-permute-done((bf16[2,4,4,32,640]{4,3,2,1,0:T(8,128)(2,1)}, bf16[2,4,4,32,640]{4,3,2,1,0:T(8,128)(2,1)}, u32[]{:S(2)}, u32[]{:S(2)}) %collective-permute-start.1) | collective-permute-done | bytes 1310752 | tf_op jit(solution)/shard_map/while/body/eval_jaxpr/ppermute | solution.py:16
  915.7 17.1 %conditional.5 = ((f32[4,10,128]{2,1,0:T(8,128)S(1)}, f32[4,10,128]{2,1,0:T(8,128)S(1)}, f32[4,10,128,64]{2,3,1,0:T(8,128)S(1)})) conditional(s32[]{:T(128)} %convert_element_type.114, (f32[4,10,128]{2,1,0:T(8,128)S(1)}, f32[4,10,128]{2,1,0:T(8,128)S(1)}, f32[4,10,128,64]{2,3,1,0:T(8,128)S(1)}) %get-tuple-element.384, ...), branch_computations={%region_17.17_spmd, %region_18.20_spmd} | conditional | flops 174018560 | bytes 28467260 | solution.py:140
  918.1 3.5 squeeze.30
  926.0 3.5 squeeze.31
  929.6 3.2 fusion.12
  937.8 21.1 %collective-permute-start = (bf16[2,4,4,32,640]{4,3,2,1,0:T(8,128)(2,1)}, bf16[2,4,4,32,640]{4,3,2,1,0:T(8,128)(2,1)}, u32[]{:S(2)}, u32[]{:S(2)}) collective-permute-start(bf16[2,4,4,32,640]{4,3,2,1,0:T(8,128)(2,1)} %get-tuple-element.365), channel_id=1, source_target_pairs={{0,8},{1,9},{2,10},{3,11},{4,12},{5,13},{6,14},{7,15},{8,16},{9,17... | collective-permute-start | bytes 3932168 | tf_op jit(solution)/shard_map/while/body/eval_jaxpr/ppermute | solution.py:16
  960.2 13.0 %collective-permute-done = bf16[2,4,4,32,640]{4,3,2,1,0:T(8,128)(2,1)} collective-permute-done((bf16[2,4,4,32,640]{4,3,2,1,0:T(8,128)(2,1)}, bf16[2,4,4,32,640]{4,3,2,1,0:T(8,128)(2,1)}, u32[]{:S(2)}, u32[]{:S(2)}) %collective-permute-start) | collective-permute-done | bytes 1310752 | tf_op jit(solution)/shard_map/while/body/eval_jaxpr/ppermute | solution.py:16
  973.2 14.5 %collective-permute-done.1 = bf16[2,4,4,32,640]{4,3,2,1,0:T(8,128)(2,1)} collective-permute-done((bf16[2,4,4,32,640]{4,3,2,1,0:T(8,128)(2,1)}, bf16[2,4,4,32,640]{4,3,2,1,0:T(8,128)(2,1)}, u32[]{:S(2)}, u32[]{:S(2)}) %collective-permute-start.1) | collective-permute-done | bytes 1310752 | tf_op jit(solution)/shard_map/while/body/eval_jaxpr/ppermute | solution.py:16
  987.7 17.1 %conditional.5 = ((f32[4,10,128]{2,1,0:T(8,128)S(1)}, f32[4,10,128]{2,1,0:T(8,128)S(1)}, f32[4,10,128,64]{2,3,1,0:T(8,128)S(1)})) conditional(s32[]{:T(128)} %convert_element_type.114, (f32[4,10,128]{2,1,0:T(8,128)S(1)}, f32[4,10,128]{2,1,0:T(8,128)S(1)}, f32[4,10,128,64]{2,3,1,0:T(8,128)S(1)}) %get-tuple-element.384, ...), branch_computations={%region_17.17_spmd, %region_18.20_spmd} | conditional | flops 174018560 | bytes 28467260 | solution.py:140
  990.2 3.5 squeeze.30
  998.1 3.5 squeeze.31
  1001.6 3.2 fusion.12
  1009.8 2.5 collective-permute-start
  1013.7 13.0 %collective-permute-done = bf16[2,4,4,32,640]{4,3,2,1,0:T(8,128)(2,1)} collective-permute-done((bf16[2,4,4,32,640]{4,3,2,1,0:T(8,128)(2,1)}, bf16[2,4,4,32,640]{4,3,2,1,0:T(8,128)(2,1)}, u32[]{:S(2)}, u32[]{:S(2)}) %collective-permute-start) | collective-permute-done | bytes 1310752 | tf_op jit(solution)/shard_map/while/body/eval_jaxpr/ppermute | solution.py:16
  1026.7 14.5 %collective-permute-done.1 = bf16[2,4,4,32,640]{4,3,2,1,0:T(8,128)(2,1)} collective-permute-done((bf16[2,4,4,32,640]{4,3,2,1,0:T(8,128)(2,1)}, bf16[2,4,4,32,640]{4,3,2,1,0:T(8,128)(2,1)}, u32[]{:S(2)}, u32[]{:S(2)}) %collective-permute-start.1) | collective-permute-done | bytes 1310752 | tf_op jit(solution)/shard_map/while/body/eval_jaxpr/ppermute | solution.py:16
  1041.2 17.1 %conditional.5 = ((f32[4,10,128]{2,1,0:T(8,128)S(1)}, f32[4,10,128]{2,1,0:T(8,128)S(1)}, f32[4,10,128,64]{2,3,1,0:T(8,128)S(1)})) conditional(s32[]{:T(128)} %convert_element_type.114, (f32[4,10,128]{2,1,0:T(8,128)S(1)}, f32[4,10,128]{2,1,0:T(8,128)S(1)}, f32[4,10,128,64]{2,3,1,0:T(8,128)S(1)}) %get-tuple-element.384, ...), branch_computations={%region_17.17_spmd, %region_18.20_spmd} | conditional | flops 174018560 | bytes 28467260 | solution.py:140
  1043.7 3.5 squeeze.30
  1051.5 3.5 squeeze.31
  1055.1 3.2 fusion.12
  1064.3 3.4 copy.68
  1067.8 3.8 dot_general.69
  (158 shorter events, 124.4 us)
Async XLA Ops:
  0.6 1072.2 %copy-start = (bf16[640,1280]{1,0:T(8,128)(2,1)S(1)}, bf16[640,1280]{1,0:T(8,128)(2,1)}, u32[]{:S(2)}) copy-start(bf16[640,1280]{1,0:T(8,128)(2,1)} %param.25) | copy-start | bytes 4915204
  0.6 10.7 copy-start.4
  0.7 2.7 copy-start.16
  4.1 556.8 %collective-permute-start.2 = (bf16[4,1,32,1280]{3,2,1,0:T(8,128)(2,1)}, bf16[4,1,32,1280]{3,2,1,0:T(8,128)(2,1)}, u32[]{:S(2)}, u32[]{:S(2)}) collective-permute-start(bf16[4,1,32,1280]{3,2,1,0:T(8,128)(2,1)} %get-tuple-element.275), channel_id=1, source_target_pairs={{0,8},{1,9},{2,10},{3,11},{4,12},{5,13},{6,14},{7,15},{8,16},{9,17... | collective-permute-start | bytes 983048 | tf_op jit(solution)/shard_map/ppermute | solution.py:16
  10.0 550.9 %collective-permute-start.3 = (bf16[4,1,32,1280]{3,2,1,0:T(8,128)(2,1)S(1)}, bf16[4,1,32,1280]{3,2,1,0:T(8,128)(2,1)}, u32[]{:S(2)}, u32[]{:S(2)}) collective-permute-start(bf16[4,1,32,1280]{3,2,1,0:T(8,128)(2,1)S(1)} %get-tuple-element.276), channel_id=1, source_target_pairs={{8,0},{9,1},{10,2},{11,3},{12,4},{13,5},{14,6},{15,7},{16,8},{17,9... | collective-permute-start | bytes 983048 | tf_op jit(solution)/shard_map/ppermute | solution.py:16
  551.7 4.2 copy-start.19
  551.7 4.5 copy-start.17
  551.7 4.5 copy-start.18
  555.9 1.4 copy-start.13
  558.1 8.4 copy-start.14
  572.4 1.7 copy-start.9
  574.1 1.3 copy-start.7
  575.5 6.4 copy-start.5
  587.9 5.9 copy-start.3
  595.9 1.6 copy-start.10
  598.2 16.7 %collective-permute-start = (bf16[2,4,4,32,640]{4,3,2,1,0:T(8,128)(2,1)}, bf16[2,4,4,32,640]{4,3,2,1,0:T(8,128)(2,1)}, u32[]{:S(2)}, u32[]{:S(2)}) collective-permute-start(bf16[2,4,4,32,640]{4,3,2,1,0:T(8,128)(2,1)} %get-tuple-element.365), channel_id=1, source_target_pairs={{0,8},{1,9},{2,10},{3,11},{4,12},{5,13},{6,14},{7,15},{8,16},{9,17... | collective-permute-start | bytes 3932168 | tf_op jit(solution)/shard_map/while/body/eval_jaxpr/ppermute | solution.py:16
  600.6 33.7 %collective-permute-start.1 = (bf16[2,4,4,32,640]{4,3,2,1,0:T(8,128)(2,1)}, bf16[2,4,4,32,640]{4,3,2,1,0:T(8,128)(2,1)}, u32[]{:S(2)}, u32[]{:S(2)}) collective-permute-start(bf16[2,4,4,32,640]{4,3,2,1,0:T(8,128)(2,1)} %get-tuple-element.366), channel_id=1, source_target_pairs={{8,0},{9,1},{10,2},{11,3},{12,4},{13,5},{14,6},{15,7},{16,8},{17,9... | collective-permute-start | bytes 3932168 | tf_op jit(solution)/shard_map/while/body/eval_jaxpr/ppermute | solution.py:16
  642.5 1.5 copy-start.2
  656.3 22.7 %collective-permute-start = (bf16[2,4,4,32,640]{4,3,2,1,0:T(8,128)(2,1)}, bf16[2,4,4,32,640]{4,3,2,1,0:T(8,128)(2,1)}, u32[]{:S(2)}, u32[]{:S(2)}) collective-permute-start(bf16[2,4,4,32,640]{4,3,2,1,0:T(8,128)(2,1)} %get-tuple-element.365), channel_id=1, source_target_pairs={{0,8},{1,9},{2,10},{3,11},{4,12},{5,13},{6,14},{7,15},{8,16},{9,17... | collective-permute-start | bytes 3932168 | tf_op jit(solution)/shard_map/while/body/eval_jaxpr/ppermute | solution.py:16
  661.1 46.6 %collective-permute-start.1 = (bf16[2,4,4,32,640]{4,3,2,1,0:T(8,128)(2,1)}, bf16[2,4,4,32,640]{4,3,2,1,0:T(8,128)(2,1)}, u32[]{:S(2)}, u32[]{:S(2)}) collective-permute-start(bf16[2,4,4,32,640]{4,3,2,1,0:T(8,128)(2,1)} %get-tuple-element.366), channel_id=1, source_target_pairs={{8,0},{9,1},{10,2},{11,3},{12,4},{13,5},{14,6},{15,7},{16,8},{17,9... | collective-permute-start | bytes 3932168 | tf_op jit(solution)/shard_map/while/body/eval_jaxpr/ppermute | solution.py:16
  716.0 1.5 copy-start.2
  729.9 19.8 %collective-permute-start = (bf16[2,4,4,32,640]{4,3,2,1,0:T(8,128)(2,1)}, bf16[2,4,4,32,640]{4,3,2,1,0:T(8,128)(2,1)}, u32[]{:S(2)}, u32[]{:S(2)}) collective-permute-start(bf16[2,4,4,32,640]{4,3,2,1,0:T(8,128)(2,1)} %get-tuple-element.365), channel_id=1, source_target_pairs={{0,8},{1,9},{2,10},{3,11},{4,12},{5,13},{6,14},{7,15},{8,16},{9,17... | collective-permute-start | bytes 3932168 | tf_op jit(solution)/shard_map/while/body/eval_jaxpr/ppermute | solution.py:16
  732.4 45.9 %collective-permute-start.1 = (bf16[2,4,4,32,640]{4,3,2,1,0:T(8,128)(2,1)}, bf16[2,4,4,32,640]{4,3,2,1,0:T(8,128)(2,1)}, u32[]{:S(2)}, u32[]{:S(2)}) collective-permute-start(bf16[2,4,4,32,640]{4,3,2,1,0:T(8,128)(2,1)} %get-tuple-element.366), channel_id=1, source_target_pairs={{8,0},{9,1},{10,2},{11,3},{12,4},{13,5},{14,6},{15,7},{16,8},{17,9... | collective-permute-start | bytes 3932168 | tf_op jit(solution)/shard_map/while/body/eval_jaxpr/ppermute | solution.py:16
  786.6 1.5 copy-start.2
  800.5 16.9 %collective-permute-start = (bf16[2,4,4,32,640]{4,3,2,1,0:T(8,128)(2,1)}, bf16[2,4,4,32,640]{4,3,2,1,0:T(8,128)(2,1)}, u32[]{:S(2)}, u32[]{:S(2)}) collective-permute-start(bf16[2,4,4,32,640]{4,3,2,1,0:T(8,128)(2,1)} %get-tuple-element.365), channel_id=1, source_target_pairs={{0,8},{1,9},{2,10},{3,11},{4,12},{5,13},{6,14},{7,15},{8,16},{9,17... | collective-permute-start | bytes 3932168 | tf_op jit(solution)/shard_map/while/body/eval_jaxpr/ppermute | solution.py:16
  803.0 41.0 %collective-permute-start.1 = (bf16[2,4,4,32,640]{4,3,2,1,0:T(8,128)(2,1)}, bf16[2,4,4,32,640]{4,3,2,1,0:T(8,128)(2,1)}, u32[]{:S(2)}, u32[]{:S(2)}) collective-permute-start(bf16[2,4,4,32,640]{4,3,2,1,0:T(8,128)(2,1)} %get-tuple-element.366), channel_id=1, source_target_pairs={{8,0},{9,1},{10,2},{11,3},{12,4},{13,5},{14,6},{15,7},{16,8},{17,9... | collective-permute-start | bytes 3932168 | tf_op jit(solution)/shard_map/while/body/eval_jaxpr/ppermute | solution.py:16
  852.3 1.5 copy-start.2
  866.1 16.9 %collective-permute-start = (bf16[2,4,4,32,640]{4,3,2,1,0:T(8,128)(2,1)}, bf16[2,4,4,32,640]{4,3,2,1,0:T(8,128)(2,1)}, u32[]{:S(2)}, u32[]{:S(2)}) collective-permute-start(bf16[2,4,4,32,640]{4,3,2,1,0:T(8,128)(2,1)} %get-tuple-element.365), channel_id=1, source_target_pairs={{0,8},{1,9},{2,10},{3,11},{4,12},{5,13},{6,14},{7,15},{8,16},{9,17... | collective-permute-start | bytes 3932168 | tf_op jit(solution)/shard_map/while/body/eval_jaxpr/ppermute | solution.py:16
  868.7 47.0 %collective-permute-start.1 = (bf16[2,4,4,32,640]{4,3,2,1,0:T(8,128)(2,1)}, bf16[2,4,4,32,640]{4,3,2,1,0:T(8,128)(2,1)}, u32[]{:S(2)}, u32[]{:S(2)}) collective-permute-start(bf16[2,4,4,32,640]{4,3,2,1,0:T(8,128)(2,1)} %get-tuple-element.366), channel_id=1, source_target_pairs={{8,0},{9,1},{10,2},{11,3},{12,4},{13,5},{14,6},{15,7},{16,8},{17,9... | collective-permute-start | bytes 3932168 | tf_op jit(solution)/shard_map/while/body/eval_jaxpr/ppermute | solution.py:16
  923.9 1.5 copy-start.2
  937.8 35.4 %collective-permute-start = (bf16[2,4,4,32,640]{4,3,2,1,0:T(8,128)(2,1)}, bf16[2,4,4,32,640]{4,3,2,1,0:T(8,128)(2,1)}, u32[]{:S(2)}, u32[]{:S(2)}) collective-permute-start(bf16[2,4,4,32,640]{4,3,2,1,0:T(8,128)(2,1)} %get-tuple-element.365), channel_id=1, source_target_pairs={{0,8},{1,9},{2,10},{3,11},{4,12},{5,13},{6,14},{7,15},{8,16},{9,17... | collective-permute-start | bytes 3932168 | tf_op jit(solution)/shard_map/while/body/eval_jaxpr/ppermute | solution.py:16
  958.9 28.8 %collective-permute-start.1 = (bf16[2,4,4,32,640]{4,3,2,1,0:T(8,128)(2,1)}, bf16[2,4,4,32,640]{4,3,2,1,0:T(8,128)(2,1)}, u32[]{:S(2)}, u32[]{:S(2)}) collective-permute-start(bf16[2,4,4,32,640]{4,3,2,1,0:T(8,128)(2,1)} %get-tuple-element.366), channel_id=1, source_target_pairs={{8,0},{9,1},{10,2},{11,3},{12,4},{13,5},{14,6},{15,7},{16,8},{17,9... | collective-permute-start | bytes 3932168 | tf_op jit(solution)/shard_map/while/body/eval_jaxpr/ppermute | solution.py:16
  996.0 1.5 copy-start.2
  1009.8 16.9 %collective-permute-start = (bf16[2,4,4,32,640]{4,3,2,1,0:T(8,128)(2,1)}, bf16[2,4,4,32,640]{4,3,2,1,0:T(8,128)(2,1)}, u32[]{:S(2)}, u32[]{:S(2)}) collective-permute-start(bf16[2,4,4,32,640]{4,3,2,1,0:T(8,128)(2,1)} %get-tuple-element.365), channel_id=1, source_target_pairs={{0,8},{1,9},{2,10},{3,11},{4,12},{5,13},{6,14},{7,15},{8,16},{9,17... | collective-permute-start | bytes 3932168 | tf_op jit(solution)/shard_map/while/body/eval_jaxpr/ppermute | solution.py:16
  1012.4 28.8 %collective-permute-start.1 = (bf16[2,4,4,32,640]{4,3,2,1,0:T(8,128)(2,1)}, bf16[2,4,4,32,640]{4,3,2,1,0:T(8,128)(2,1)}, u32[]{:S(2)}, u32[]{:S(2)}) collective-permute-start(bf16[2,4,4,32,640]{4,3,2,1,0:T(8,128)(2,1)} %get-tuple-element.366), channel_id=1, source_target_pairs={{8,0},{9,1},{10,2},{11,3},{12,4},{13,5},{14,6},{15,7},{16,8},{17,9... | collective-permute-start | bytes 3932168 | tf_op jit(solution)/shard_map/while/body/eval_jaxpr/ppermute | solution.py:16
  1049.4 1.5 copy-start.2
  1067.8 3.8 copy-start.11
  1067.8 3.8 copy-start.12
  1071.6 1.2 copy-start.6
  1071.6 1.8 copy-start.8
  1071.6 2.0 copy-start.15
